TPU v7x, 32 devices: a whole 2x2x4 slice. The times are simulated.
32 devices in a mesh: dp: 4 (over y, core), blk: 8 (over z, x).
Axes of the slice: x: 2, y: 2, z: 4, core: 2. Of those that a mesh axis runs over, the one named last changes fastest.
Arguments:
- pre_gelu: bfloat16 [6144, 4096], P(('dp', 'blk')), may hold values from -8 to 8
- out_grad: bfloat16 [6144, 1024], P(('dp', 'blk')), may hold values from -6 to 6
- down_weight: bfloat16 [4096, 1024], P('blk'), may hold values from -0.09375 to 0.09375
Outputs:
- block_out: bfloat16 [6144, 1024], P(('dp', 'blk'))
- pre_grad: bfloat16 [6144, 4096], P(('dp', 'blk'))
- weight_grad: float32 [4096, 1024], P('blk')
All inputs are finite; a program needn't handle non-finite values.
Results may differ from a plain program's by a relative error of at most 0.017.
Values may be sent and summed in bfloat16 or wider, within the bound.
No kernel may reach another device: no remote copies, remote signals or barrier semaphores. Data moves between devices by JAX's collectives and lax.ppermute only.
A program may use at most 64 MiB of HBM per device.

v0:
```python
import math
import jax
import jax.numpy as jnp
from jax import lax
from jax.sharding import PartitionSpec as P

SQRT_TWO_PI = 0.7978845608028654
CUBIC = 0.044715


def passed_along(array, axis, by):
    peers = lax.axis_size(axis)
    return lax.ppermute(array, axis, [(i, (i + by) % peers) for i in range(peers)])


def gelu_parts(inputs):
    argument = SQRT_TWO_PI * (inputs + CUBIC * inputs * inputs * inputs)
    tangent = jnp.tanh(argument)
    activation = 0.5 * inputs * (1.0 + tangent)
    derivative = 0.5 * (1.0 + tangent) + 0.5 * inputs * (1.0 - tangent * tangent) * SQRT_TWO_PI * (
        1.0 + 3.0 * CUBIC * inputs * inputs
    )
    return (activation, derivative)


def finish_partial(arrived, own_term):
    rounded = (arrived.astype(jnp.float32) + own_term).astype(jnp.bfloat16)
    return lax.optimization_barrier(rounded).astype(jnp.float32)


def body(pre_gelu, out_grad, down_weight):
    row_count = pre_gelu.shape[0]
    block_rows = down_weight.shape[0]
    cycle_size = lax.axis_size("blk")
    home_index = lax.axis_index("blk")
    activation, derivative = gelu_parts(pre_gelu.astype(jnp.float32))
    hidden = activation.astype(jnp.bfloat16)
    weights_all = lax.all_gather(down_weight, "blk", axis=0, tiled=True)
    out_total = jnp.dot(hidden, weights_all, preferred_element_type=jnp.float32)
    d_hidden = lax.dot_general(
        out_grad, weights_all, (((1,), (1,)), ((), ())), preferred_element_type=jnp.float32
    )
    grad_buffer = (d_hidden * derivative).astype(jnp.bfloat16)

    def block_term(block_index):
        hidden_part = lax.dynamic_slice_in_dim(hidden, block_index * block_rows, block_rows, 1)
        return lax.dot_general(
            hidden_part, out_grad, (((0,), (0,)), ((), ())), preferred_element_type=jnp.float32
        )

    def pass_chain(partial_value):
        return passed_along(partial_value, "blk", 1)

    own_term = block_term(home_index)
    partial_value = block_term(jnp.mod(home_index - 1, cycle_size)).astype(jnp.bfloat16)

    def chain_stop(stop_number, partial_value):
        contribution = block_term(jnp.mod(home_index - stop_number, cycle_size))
        return (pass_chain(partial_value).astype(jnp.float32) + contribution).astype(jnp.bfloat16)

    partial_value = lax.fori_loop(2, cycle_size, chain_stop, partial_value)
    finished = finish_partial(pass_chain(partial_value), own_term)
    summed = lax.psum(finished.astype(jnp.bfloat16), "dp").astype(jnp.float32)
    token_count = row_count * cycle_size * lax.axis_size("dp")
    return (out_total.astype(jnp.bfloat16), grad_buffer, summed / math.sqrt(token_count))


def solution(mesh):
    in_specs = (P(("dp", "blk"), None), P(("dp", "blk"), None), P("blk", None))
    out_specs = (P(("dp", "blk"), None), P(("dp", "blk"), None), P("blk", None))
    return jax.shard_map(body, mesh=mesh, in_specs=in_specs, out_specs=out_specs, check_vma=False)
```

profile of v0, /device:TPU:0, one launch (start us, length us, event | category | flops | bytes accessed | tf_op | source)
XLA Modules:
  0.0 344.3 jit_solution(13820292704655213971)
XLA Ops:
  8.0 0.0 all-reduce.2.cloned.1.call-start
  8.1 2.5 fusion.8
  10.6 1.5 convolution_convert_fusion
  12.1 165.6 %while.15 = (s32[]{:T(128)}, bf16[512,1024]{1,0:T(8,128)(2,1)}, s32[]{:T(128)}, bf16[192,4096]{1,0:T(8,128)(2,1)S(1)}, bf16[192,1024]{1,0:T(8,128)(2,1)S(1)}, /*...) while((s32[]{:T(128)}, bf16[512,1024]{1,0:T(8,128)(2,1)}, ...), condition=%wide.region_1.2_spmd, body=%wide.region_0.1_spmd.sunk | while | flops 202899472 | bytes 6881620 | solution.py:61
  12.1 3.0 collective-permute-start
  15.0 26.4 %collective-permute-done = bf16[512,1024]{1,0:T(8,128)(2,1)S(1)} collective-permute-done((bf16[512,1024]{1,0:T(8,128)(2,1)}, bf16[512,1024]{1,0:T(8,128)(2,1)S(1)}, u32[]{:S(2)}, u32[]{:S(2)}) %collective-permute-start) | collective-permute-done | bytes 1048608 | tf_op jit(solution)/shard_map/while/body/eval_jaxpr/ppermute | solution.py:13
  41.4 1.4 add_convert_fusion.3
  42.9 0.0 collective-permute-start
  42.9 27.2 %collective-permute-done = bf16[512,1024]{1,0:T(8,128)(2,1)S(1)} collective-permute-done((bf16[512,1024]{1,0:T(8,128)(2,1)}, bf16[512,1024]{1,0:T(8,128)(2,1)S(1)}, u32[]{:S(2)}, u32[]{:S(2)}) %collective-permute-start) | collective-permute-done | bytes 1048608 | tf_op jit(solution)/shard_map/while/body/eval_jaxpr/ppermute | solution.py:13
  70.1 1.4 add_convert_fusion.3
  71.6 0.0 collective-permute-start
  71.6 26.4 %collective-permute-done = bf16[512,1024]{1,0:T(8,128)(2,1)S(1)} collective-permute-done((bf16[512,1024]{1,0:T(8,128)(2,1)}, bf16[512,1024]{1,0:T(8,128)(2,1)S(1)}, u32[]{:S(2)}, u32[]{:S(2)}) %collective-permute-start) | collective-permute-done | bytes 1048608 | tf_op jit(solution)/shard_map/while/body/eval_jaxpr/ppermute | solution.py:13
  97.9 1.4 add_convert_fusion.3
  99.4 0.0 collective-permute-start
  99.4 25.5 %collective-permute-done = bf16[512,1024]{1,0:T(8,128)(2,1)S(1)} collective-permute-done((bf16[512,1024]{1,0:T(8,128)(2,1)}, bf16[512,1024]{1,0:T(8,128)(2,1)S(1)}, u32[]{:S(2)}, u32[]{:S(2)}) %collective-permute-start) | collective-permute-done | bytes 1048608 | tf_op jit(solution)/shard_map/while/body/eval_jaxpr/ppermute | solution.py:13
  124.9 1.4 add_convert_fusion.3
  126.3 24.7 %collective-permute-done = bf16[512,1024]{1,0:T(8,128)(2,1)S(1)} collective-permute-done((bf16[512,1024]{1,0:T(8,128)(2,1)}, bf16[512,1024]{1,0:T(8,128)(2,1)S(1)}, u32[]{:S(2)}, u32[]{:S(2)}) %collective-permute-start) | collective-permute-done | bytes 1048608 | tf_op jit(solution)/shard_map/while/body/eval_jaxpr/ppermute | solution.py:13
  151.0 1.4 add_convert_fusion.3
  152.4 0.0 collective-permute-start
  152.4 23.8 %collective-permute-done = bf16[512,1024]{1,0:T(8,128)(2,1)S(1)} collective-permute-done((bf16[512,1024]{1,0:T(8,128)(2,1)}, bf16[512,1024]{1,0:T(8,128)(2,1)S(1)}, u32[]{:S(2)}, u32[]{:S(2)}) %collective-permute-start) | collective-permute-done | bytes 1048608 | tf_op jit(solution)/shard_map/while/body/eval_jaxpr/ppermute | solution.py:13
  176.3 1.4 add_convert_fusion.3
  177.7 0.0 collective-permute-start.1
  177.7 23.0 %collective-permute-done.1 = bf16[512,1024]{1,0:T(8,128)(2,1)S(1)} collective-permute-done((bf16[512,1024]{1,0:T(8,128)(2,1)}, bf16[512,1024]{1,0:T(8,128)(2,1)S(1)}, u32[]{:S(2)}, u32[]{:S(2)}) %collective-permute-start.1) | collective-permute-done | bytes 1048608 | tf_op jit(solution)/shard_map/ppermute | solution.py:13
  200.7 1.4 add_convert_fusion.1
  202.1 0.0 all-reduce.2.cloned.1.call-update
  202.1 0.0 all-gather.2.cloned.1.call-start
  202.2 0.5 all-gather.2.cloned.1.call-update
  202.7 32.3 %all-reduce.2.cloned.1.call-done = bf16[512,1024]{1,0:T(8,128)(2,1)} async-done(((bf16[512,1024]{1,0:T(8,128)(2,1)}), bf16[512,1024]{1,0:T(8,128)(2,1)}) %all-reduce.2.cloned.1.call-update) | async-done | bytes 1048592 | tf_op jit(solution)/shard_map/psum | solution.py:63
  235.0 2.8 convert_multiply_fusion.6
  237.8 87.2 %all-gather.2.cloned.1.call-done = bf16[4096,1024]{1,0:T(8,128)(2,1)} async-done(((bf16[512,1024]{1,0:T(8,128)(2,1)}), bf16[4096,1024]{1,0:T(8,128)(2,1)}) %all-gather.2.cloned.1.call-update) | async-done | bytes 8388624 | tf_op jit(solution)/shard_map/all_gather | solution.py:38
  325.0 6.5 %convolution_convert_fusion.1 = bf16[192,1024]{1,0:T(8,128)(2,1)} fusion(bf16[4096,1024]{1,0:T(8,128)(2,1)} %all-gather.2.cloned.1.call-done, bf16[192,4096]{1,0:T(8,128)(2,1)S(1)} %copy-done.1), kind=kOutput, calls=%fused_computation.25 | convolution fusion | flops 1618673664 | bytes 10354688 | tf_op jit(solution)/shard_map/dot_general | solution.py:39
  331.5 5.3 %fusion.5 = bf16[192,4096]{1,0:T(8,128)(2,1)} fusion(bf16[192,1024]{1,0:T(8,128)(2,1)S(1)} %get-tuple-element.217, bf16[4096,1024]{1,0:T(8,128)(2,1)S(1)} %copy-done.2, bf16[192,4096]{1,0:T(8,128)(2,1)S(1)} %copy-done.1), kind=kOutput, calls=%fused_computation.12 | convolution fusion | flops 1626341376 | bytes 11927552 | tf_op jit(solution)/shard_map/dot_general | solution.py:40
  (7 shorter events, 0.0 us)
Async XLA Ops:
  8.0 2.6 copy-start
  8.0 227.0 %all-reduce.2.cloned.1.call-start = ((), (), s32[]{:S(2)}) async-start(), calls=%async_computation.1 | async-start | bytes 2097152 | tf_op jit(solution)/shard_map/psum | solution.py:63
  12.1 29.4 %collective-permute-start = (bf16[512,1024]{1,0:T(8,128)(2,1)}, bf16[512,1024]{1,0:T(8,128)(2,1)S(1)}, u32[]{:S(2)}, u32[]{:S(2)}) collective-permute-start(bf16[512,1024]{1,0:T(8,128)(2,1)} %get-tuple-element.191), channel_id=1, source_target_pairs={{0,1},{1,2},{2,3},{3,4},{4,5},{5,6},{6,7},{7,0},{8,9},{9,10},{10,1... | collective-permute-start | bytes 3145736 | tf_op jit(solution)/shard_map/while/body/eval_jaxpr/ppermute | solution.py:13
  42.9 27.2 %collective-permute-start = (bf16[512,1024]{1,0:T(8,128)(2,1)}, bf16[512,1024]{1,0:T(8,128)(2,1)S(1)}, u32[]{:S(2)}, u32[]{:S(2)}) collective-permute-start(bf16[512,1024]{1,0:T(8,128)(2,1)} %get-tuple-element.191), channel_id=1, source_target_pairs={{0,1},{1,2},{2,3},{3,4},{4,5},{5,6},{6,7},{7,0},{8,9},{9,10},{10,1... | collective-permute-start | bytes 3145736 | tf_op jit(solution)/shard_map/while/body/eval_jaxpr/ppermute | solution.py:13
  71.6 26.4 %collective-permute-start = (bf16[512,1024]{1,0:T(8,128)(2,1)}, bf16[512,1024]{1,0:T(8,128)(2,1)S(1)}, u32[]{:S(2)}, u32[]{:S(2)}) collective-permute-start(bf16[512,1024]{1,0:T(8,128)(2,1)} %get-tuple-element.191), channel_id=1, source_target_pairs={{0,1},{1,2},{2,3},{3,4},{4,5},{5,6},{6,7},{7,0},{8,9},{9,10},{10,1... | collective-permute-start | bytes 3145736 | tf_op jit(solution)/shard_map/while/body/eval_jaxpr/ppermute | solution.py:13
  99.4 25.5 %collective-permute-start = (bf16[512,1024]{1,0:T(8,128)(2,1)}, bf16[512,1024]{1,0:T(8,128)(2,1)S(1)}, u32[]{:S(2)}, u32[]{:S(2)}) collective-permute-start(bf16[512,1024]{1,0:T(8,128)(2,1)} %get-tuple-element.191), channel_id=1, source_target_pairs={{0,1},{1,2},{2,3},{3,4},{4,5},{5,6},{6,7},{7,0},{8,9},{9,10},{10,1... | collective-permute-start | bytes 3145736 | tf_op jit(solution)/shard_map/while/body/eval_jaxpr/ppermute | solution.py:13
  126.3 24.7 %collective-permute-start = (bf16[512,1024]{1,0:T(8,128)(2,1)}, bf16[512,1024]{1,0:T(8,128)(2,1)S(1)}, u32[]{:S(2)}, u32[]{:S(2)}) collective-permute-start(bf16[512,1024]{1,0:T(8,128)(2,1)} %get-tuple-element.191), channel_id=1, source_target_pairs={{0,1},{1,2},{2,3},{3,4},{4,5},{5,6},{6,7},{7,0},{8,9},{9,10},{10,1... | collective-permute-start | bytes 3145736 | tf_op jit(solution)/shard_map/while/body/eval_jaxpr/ppermute | solution.py:13
  152.4 23.8 %collective-permute-start = (bf16[512,1024]{1,0:T(8,128)(2,1)}, bf16[512,1024]{1,0:T(8,128)(2,1)S(1)}, u32[]{:S(2)}, u32[]{:S(2)}) collective-permute-start(bf16[512,1024]{1,0:T(8,128)(2,1)} %get-tuple-element.191), channel_id=1, source_target_pairs={{0,1},{1,2},{2,3},{3,4},{4,5},{5,6},{6,7},{7,0},{8,9},{9,10},{10,1... | collective-permute-start | bytes 3145736 | tf_op jit(solution)/shard_map/while/body/eval_jaxpr/ppermute | solution.py:13
  177.7 23.0 %collective-permute-start.1 = (bf16[512,1024]{1,0:T(8,128)(2,1)}, bf16[512,1024]{1,0:T(8,128)(2,1)S(1)}, u32[]{:S(2)}, u32[]{:S(2)}) collective-permute-start(bf16[512,1024]{1,0:T(8,128)(2,1)} %get-tuple-element.136), channel_id=1, source_target_pairs={{0,1},{1,2},{2,3},{3,4},{4,5},{5,6},{6,7},{7,0},{8,9},{9,10},{10,1... | collective-permute-start | bytes 3145736 | tf_op jit(solution)/shard_map/ppermute | solution.py:13
  202.1 122.9 %copy-start.1 = (bf16[192,4096]{1,0:T(8,128)(2,1)S(1)}, bf16[192,4096]{1,0:T(8,128)(2,1)}, u32[]{:S(2)}) copy-start(bf16[192,4096]{1,0:T(8,128)(2,1)} %param.5) | copy-start | bytes 4718596
  202.1 122.9 %all-gather.2.cloned.1.call-start = ((), (), s32[]{:S(2)}) async-start(), calls=%async_computation | async-start | bytes 9437184 | tf_op jit(solution)/shard_map/all_gather | solution.py:38
  325.0 6.5 %copy-start.2 = (bf16[4096,1024]{1,0:T(8,128)(2,1)S(1)}, bf16[4096,1024]{1,0:T(8,128)(2,1)}, u32[]{:S(2)}) copy-start(bf16[4096,1024]{1,0:T(8,128)(2,1)} %all-gather.2.cloned.1.call-done) | copy-start | bytes 25165828
Sparse Core Ops, SparseCore 0:
  202.2 32.6 all-reduce.1
Sparse Core Ops, SparseCore 1:
  204.7 120.2 all-gather.1
where the time goes:
time: 344 us
  waiting for transfers between devices  297 us (86%)
  matrix products  23.3 us (7%)
  between operations  15.5 us (5%)
  other arithmetic  5.35 us (2%)
    ppermute x7, waiting for transfers between devices, passed_along(): lax.ppermute(array, axis, [(i, (i + by) % peers) for i in range(peers)])  177 us
    all_gather x1, waiting for transfers between devices, body(): weights_all = lax.all_gather(down_weight, 'blk', axis=0, tiled=True)  87.2 us
    psum x1, waiting for transfers between devices, body(): summed = lax.psum(finished.astype(jnp.bfloat16), 'dp').astype(jnp.float32)  32.3 us
    dot_general x8, matrix products, block_term(): lax.dot_general(hidden_part, out_grad, (((0,), (0,)), ((), ())), preferre...  11.6 us
  transfers between devices with their start and end apart: 9, of which 9 were waited for; matrix products, arithmetic and copies ran while one was open for 1% of the time, Pallas kernels for 0%

commit v1 on v0

--- a/solution.py
+++ b/solution.py
@@ -3,6 +3,7 @@
 import jax.numpy as jnp
 from jax import lax
 from jax.sharding import PartitionSpec as P
+from jax.lax import all_gather
 
 SQRT_TWO_PI = 0.7978845608028654
 CUBIC = 0.044715
@@ -29,6 +30,10 @@
 
 
 def body(pre_gelu, out_grad, down_weight):
+
+    def supply_all_outputs(obj, mesh_dim):
+        return all_gather(obj, axis_name=mesh_dim).sum(axis=0)
+
     row_count = pre_gelu.shape[0]
     block_rows = down_weight.shape[0]
     cycle_size = lax.axis_size("blk")
@@ -60,7 +65,7 @@
 
     partial_value = lax.fori_loop(2, cycle_size, chain_stop, partial_value)
     finished = finish_partial(pass_chain(partial_value), own_term)
-    summed = lax.psum(finished.astype(jnp.bfloat16), "dp").astype(jnp.float32)
+    summed = supply_all_outputs(finished.astype(jnp.bfloat16), "dp").astype(jnp.float32)
     token_count = row_count * cycle_size * lax.axis_size("dp")
     return (out_total.astype(jnp.bfloat16), grad_buffer, summed / math.sqrt(token_count))
 

time: 344 us -> 377 us (1.096)
  waiting for transfers between devices: 297 us -> 329 us
    all_gather x1, waiting for transfers between devices: 87.2 us -> 122 us  [body(): weights_all = lax.all_gather(down_weight, 'blk', axis=0, tiled=True)]
    psum x1 -> x0, waiting for transfers between devices: 32.3 us -> none  [body(): summed = lax.psum(finished.astype(jnp.bfloat16), 'dp').astype(jnp.float32)]
    all_gather x0 -> x1, waiting for transfers between devices: none -> 30 us  [supply_all_outputs(): return all_gather(obj, axis_name=mesh_dim).sum(axis=0)]
where the time goes in v1:
time: 377 us
  waiting for transfers between devices  329 us (87%)
  matrix products  23.3 us (6%)
  between operations  14.1 us (4%)
  other arithmetic  7.56 us (2%)
    ppermute x7, waiting for transfers between devices, passed_along(): lax.ppermute(array, axis, [(i, (i + by) % peers) for i in range(peers)])  177 us
    all_gather x1, waiting for transfers between devices, body(): weights_all = lax.all_gather(down_weight, 'blk', axis=0, tiled=True)  122 us
    all_gather x1, waiting for transfers between devices, supply_all_outputs(): return all_gather(obj, axis_name=mesh_dim).sum(axis=0)  30 us
    dot_general x8, matrix products, block_term(): lax.dot_general(hidden_part, out_grad, (((0,), (0,)), ((), ())), preferre...  11.6 us
  transfers between devices with their start and end apart: 9, of which 9 were waited for; matrix products, arithmetic and copies ran while one was open for 1% of the time, Pallas kernels for 0%

profile of v1, /device:TPU:0, one launch (start us, length us, event | category | flops | bytes accessed | tf_op | source)
XLA Modules:
  0.0 377.3 jit_solution(7196080881786498649)
XLA Ops:
  7.2 0.0 all-gather.6.cloned.1.call-start
  7.2 2.5 fusion.8
  9.8 1.5 convolution_convert_fusion
  11.2 165.6 %while.15 = (s32[]{:T(128)}, bf16[512,1024]{1,0:T(8,128)(2,1)}, s32[]{:T(128)}, bf16[192,4096]{1,0:T(8,128)(2,1)S(1)}, bf16[192,1024]{1,0:T(8,128)(2,1)S(1)}, /*...) while((s32[]{:T(128)}, bf16[512,1024]{1,0:T(8,128)(2,1)}, ...), condition=%wide.region_1.2_spmd, body=%wide.region_0.1_spmd.sunk | while | flops 202899472 | bytes 6881620 | solution.py:66
  11.2 3.0 collective-permute-start
  14.2 26.4 %collective-permute-done = bf16[512,1024]{1,0:T(8,128)(2,1)S(1)} collective-permute-done((bf16[512,1024]{1,0:T(8,128)(2,1)}, bf16[512,1024]{1,0:T(8,128)(2,1)S(1)}, u32[]{:S(2)}, u32[]{:S(2)}) %collective-permute-start) | collective-permute-done | bytes 1048608 | tf_op jit(solution)/shard_map/while/body/eval_jaxpr/ppermute | solution.py:14
  40.6 1.4 add_convert_fusion.3
  42.0 0.0 collective-permute-start
  42.0 27.2 %collective-permute-done = bf16[512,1024]{1,0:T(8,128)(2,1)S(1)} collective-permute-done((bf16[512,1024]{1,0:T(8,128)(2,1)}, bf16[512,1024]{1,0:T(8,128)(2,1)S(1)}, u32[]{:S(2)}, u32[]{:S(2)}) %collective-permute-start) | collective-permute-done | bytes 1048608 | tf_op jit(solution)/shard_map/while/body/eval_jaxpr/ppermute | solution.py:14
  69.3 1.4 add_convert_fusion.3
  70.7 0.0 collective-permute-start
  70.7 26.4 %collective-permute-done = bf16[512,1024]{1,0:T(8,128)(2,1)S(1)} collective-permute-done((bf16[512,1024]{1,0:T(8,128)(2,1)}, bf16[512,1024]{1,0:T(8,128)(2,1)S(1)}, u32[]{:S(2)}, u32[]{:S(2)}) %collective-permute-start) | collective-permute-done | bytes 1048608 | tf_op jit(solution)/shard_map/while/body/eval_jaxpr/ppermute | solution.py:14
  97.1 1.4 add_convert_fusion.3
  98.6 25.5 %collective-permute-done = bf16[512,1024]{1,0:T(8,128)(2,1)S(1)} collective-permute-done((bf16[512,1024]{1,0:T(8,128)(2,1)}, bf16[512,1024]{1,0:T(8,128)(2,1)S(1)}, u32[]{:S(2)}, u32[]{:S(2)}) %collective-permute-start) | collective-permute-done | bytes 1048608 | tf_op jit(solution)/shard_map/while/body/eval_jaxpr/ppermute | solution.py:14
  124.1 1.4 add_convert_fusion.3
  125.5 24.7 %collective-permute-done = bf16[512,1024]{1,0:T(8,128)(2,1)S(1)} collective-permute-done((bf16[512,1024]{1,0:T(8,128)(2,1)}, bf16[512,1024]{1,0:T(8,128)(2,1)S(1)}, u32[]{:S(2)}, u32[]{:S(2)}) %collective-permute-start) | collective-permute-done | bytes 1048608 | tf_op jit(solution)/shard_map/while/body/eval_jaxpr/ppermute | solution.py:14
  150.2 1.4 add_convert_fusion.3
  151.6 0.0 collective-permute-start
  151.6 23.8 %collective-permute-done = bf16[512,1024]{1,0:T(8,128)(2,1)S(1)} collective-permute-done((bf16[512,1024]{1,0:T(8,128)(2,1)}, bf16[512,1024]{1,0:T(8,128)(2,1)S(1)}, u32[]{:S(2)}, u32[]{:S(2)}) %collective-permute-start) | collective-permute-done | bytes 1048608 | tf_op jit(solution)/shard_map/while/body/eval_jaxpr/ppermute | solution.py:14
  175.4 1.4 add_convert_fusion.3
  176.9 0.0 collective-permute-start.1
  176.9 22.9 %collective-permute-done.1 = bf16[512,1024]{1,0:T(8,128)(2,1)S(1)} collective-permute-done((bf16[512,1024]{1,0:T(8,128)(2,1)}, bf16[512,1024]{1,0:T(8,128)(2,1)S(1)}, u32[]{:S(2)}, u32[]{:S(2)}) %collective-permute-start.1) | collective-permute-done | bytes 1048608 | tf_op jit(solution)/shard_map/ppermute | solution.py:14
  199.8 1.4 add_convert_fusion.1
  201.2 0.0 all-gather.6.cloned.1.call-update
  201.3 0.0 all-gather.4.cloned.1.call-start
  201.3 0.7 all-gather.4.cloned.1.call-update
  202.0 30.0 %all-gather.6.cloned.1.call-done = bf16[2048,1024]{1,0:T(8,128)(2,1)} async-done(((bf16[512,1024]{1,0:T(8,128)(2,1)}), bf16[2048,1024]{1,0:T(8,128)(2,1)}) %all-gather.6.cloned.1.call-update) | async-done | bytes 4194320 | tf_op jit(solution)/shard_map/all_gather | solution.py:35
  232.0 3.4 reduce_sum.12
  235.5 1.6 convert_multiply_fusion.6
  237.1 121.6 %all-gather.4.cloned.1.call-done = bf16[4096,1024]{1,0:T(8,128)(2,1)} async-done(((bf16[512,1024]{1,0:T(8,128)(2,1)}), bf16[4096,1024]{1,0:T(8,128)(2,1)}) %all-gather.4.cloned.1.call-update) | async-done | bytes 8388624 | tf_op jit(solution)/shard_map/all_gather | solution.py:43
  358.6 6.5 %convolution_convert_fusion.1 = bf16[192,1024]{1,0:T(8,128)(2,1)} fusion(bf16[4096,1024]{1,0:T(8,128)(2,1)} %all-gather.4.cloned.1.call-done, bf16[192,4096]{1,0:T(8,128)(2,1)S(1)} %copy-done.1), kind=kOutput, calls=%fused_computation.25 | convolution fusion | flops 1618673664 | bytes 10354688 | tf_op jit(solution)/shard_map/dot_general | solution.py:44
  365.1 5.3 %fusion.5 = bf16[192,4096]{1,0:T(8,128)(2,1)} fusion(bf16[192,1024]{1,0:T(8,128)(2,1)S(1)} %get-tuple-element.217, bf16[4096,1024]{1,0:T(8,128)(2,1)S(1)} %copy-done.2, bf16[192,4096]{1,0:T(8,128)(2,1)S(1)} %copy-done.1), kind=kOutput, calls=%fused_computation.12 | convolution fusion | flops 1626341376 | bytes 11927552 | tf_op jit(solution)/shard_map/dot_general | solution.py:45
  (8 shorter events, 0.0 us)
Async XLA Ops:
  7.2 2.6 copy-start
  7.2 224.8 %all-gather.6.cloned.1.call-start = ((), (), s32[]{:S(2)}) async-start(), calls=%async_computation.1 | async-start | bytes 5242880 | tf_op jit(solution)/shard_map/all_gather | solution.py:35
  11.2 29.4 %collective-permute-start = (bf16[512,1024]{1,0:T(8,128)(2,1)}, bf16[512,1024]{1,0:T(8,128)(2,1)S(1)}, u32[]{:S(2)}, u32[]{:S(2)}) collective-permute-start(bf16[512,1024]{1,0:T(8,128)(2,1)} %get-tuple-element.191), channel_id=1, source_target_pairs={{0,1},{1,2},{2,3},{3,4},{4,5},{5,6},{6,7},{7,0},{8,9},{9,10},{10,1... | collective-permute-start | bytes 3145736 | tf_op jit(solution)/shard_map/while/body/eval_jaxpr/ppermute | solution.py:14
  42.0 27.2 %collective-permute-start = (bf16[512,1024]{1,0:T(8,128)(2,1)}, bf16[512,1024]{1,0:T(8,128)(2,1)S(1)}, u32[]{:S(2)}, u32[]{:S(2)}) collective-permute-start(bf16[512,1024]{1,0:T(8,128)(2,1)} %get-tuple-element.191), channel_id=1, source_target_pairs={{0,1},{1,2},{2,3},{3,4},{4,5},{5,6},{6,7},{7,0},{8,9},{9,10},{10,1... | collective-permute-start | bytes 3145736 | tf_op jit(solution)/shard_map/while/body/eval_jaxpr/ppermute | solution.py:14
  70.7 26.4 %collective-permute-start = (bf16[512,1024]{1,0:T(8,128)(2,1)}, bf16[512,1024]{1,0:T(8,128)(2,1)S(1)}, u32[]{:S(2)}, u32[]{:S(2)}) collective-permute-start(bf16[512,1024]{1,0:T(8,128)(2,1)} %get-tuple-element.191), channel_id=1, source_target_pairs={{0,1},{1,2},{2,3},{3,4},{4,5},{5,6},{6,7},{7,0},{8,9},{9,10},{10,1... | collective-permute-start | bytes 3145736 | tf_op jit(solution)/shard_map/while/body/eval_jaxpr/ppermute | solution.py:14
  98.6 25.5 %collective-permute-start = (bf16[512,1024]{1,0:T(8,128)(2,1)}, bf16[512,1024]{1,0:T(8,128)(2,1)S(1)}, u32[]{:S(2)}, u32[]{:S(2)}) collective-permute-start(bf16[512,1024]{1,0:T(8,128)(2,1)} %get-tuple-element.191), channel_id=1, source_target_pairs={{0,1},{1,2},{2,3},{3,4},{4,5},{5,6},{6,7},{7,0},{8,9},{9,10},{10,1... | collective-permute-start | bytes 3145736 | tf_op jit(solution)/shard_map/while/body/eval_jaxpr/ppermute | solution.py:14
  125.5 24.7 %collective-permute-start = (bf16[512,1024]{1,0:T(8,128)(2,1)}, bf16[512,1024]{1,0:T(8,128)(2,1)S(1)}, u32[]{:S(2)}, u32[]{:S(2)}) collective-permute-start(bf16[512,1024]{1,0:T(8,128)(2,1)} %get-tuple-element.191), channel_id=1, source_target_pairs={{0,1},{1,2},{2,3},{3,4},{4,5},{5,6},{6,7},{7,0},{8,9},{9,10},{10,1... | collective-permute-start | bytes 3145736 | tf_op jit(solution)/shard_map/while/body/eval_jaxpr/ppermute | solution.py:14
  151.6 23.8 %collective-permute-start = (bf16[512,1024]{1,0:T(8,128)(2,1)}, bf16[512,1024]{1,0:T(8,128)(2,1)S(1)}, u32[]{:S(2)}, u32[]{:S(2)}) collective-permute-start(bf16[512,1024]{1,0:T(8,128)(2,1)} %get-tuple-element.191), channel_id=1, source_target_pairs={{0,1},{1,2},{2,3},{3,4},{4,5},{5,6},{6,7},{7,0},{8,9},{9,10},{10,1... | collective-permute-start | bytes 3145736 | tf_op jit(solution)/shard_map/while/body/eval_jaxpr/ppermute | solution.py:14
  176.9 22.9 %collective-permute-start.1 = (bf16[512,1024]{1,0:T(8,128)(2,1)}, bf16[512,1024]{1,0:T(8,128)(2,1)S(1)}, u32[]{:S(2)}, u32[]{:S(2)}) collective-permute-start(bf16[512,1024]{1,0:T(8,128)(2,1)} %get-tuple-element.136), channel_id=1, source_target_pairs={{0,1},{1,2},{2,3},{3,4},{4,5},{5,6},{6,7},{7,0},{8,9},{9,10},{10,1... | collective-permute-start | bytes 3145736 | tf_op jit(solution)/shard_map/ppermute | solution.py:14
  201.3 157.4 %all-gather.4.cloned.1.call-start = ((), (), s32[]{:S(2)}) async-start(), calls=%async_computation | async-start | bytes 9437184 | tf_op jit(solution)/shard_map/all_gather | solution.py:43
  232.0 126.6 %copy-start.1 = (bf16[192,4096]{1,0:T(8,128)(2,1)S(1)}, bf16[192,4096]{1,0:T(8,128)(2,1)}, u32[]{:S(2)}) copy-start(bf16[192,4096]{1,0:T(8,128)(2,1)} %param.5) | copy-start | bytes 4718596
  358.6 6.5 %copy-start.2 = (bf16[4096,1024]{1,0:T(8,128)(2,1)S(1)}, bf16[4096,1024]{1,0:T(8,128)(2,1)}, u32[]{:S(2)}) copy-start(bf16[4096,1024]{1,0:T(8,128)(2,1)} %all-gather.4.cloned.1.call-done) | copy-start | bytes 25165828
Sparse Core Ops, SparseCore 0:
  201.4 30.5 all-gather.5
  234.1 124.4 all-gather.3
